TPU v7x, 32 devices: a whole 2x2x4 slice. The times are simulated.
32 devices in a mesh: group: 2 (over y), row: 8 (over z, x), col: 2 (over core).
Axes of the slice: x: 2, y: 2, z: 4, core: 2. Of those that a mesh axis runs over, the one named last changes fastest.
Arguments:
- map_in: bfloat16 [192, 96, 48], P(('group', 'row'), 'col'), parts along dimension 0, may hold values from -6 to 6
- embedding: bfloat16 [192, 96], P(('group', 'row')), parts along dimension 0, may hold values from -6 to 6
- w_row: bfloat16 [96, 48], replicated, may hold values from -0.625 to 0.625
- w_col: bfloat16 [96, 48], replicated, may hold values from -0.625 to 0.625
- first_kernel_weight: bfloat16 [3, 3, 48, 48], replicated, may hold values from -0.3125 to 0.3125
- first_bias: float32 [48], replicated, may hold values from -0.5 to 0.5
- second_kernel_weight: bfloat16 [3, 3, 48, 48], replicated, may hold values from -0.3125 to 0.3125
- second_bias: float32 [48], replicated, may hold values from -0.5 to 0.5
- w_mix: bfloat16 [48, 48], replicated, may hold values from -0.875 to 0.875
- b_mix: float32 [48], replicated, may hold values from -0.5 to 0.5
- w_head: float32 [48], replicated, may hold values from -0.875 to 0.875
Outputs:
- contacts: float32 [192, 96], P(('group', 'row'), 'col'), parts along dimension 0
There are 2 independent parts, one for each index of `group`. A program takes and returns all parts, laid end to end along the dimension named above; an argument that names none is the same for every part. Nothing has to cross between parts.
All inputs are finite; a program needn't handle non-finite values.
Results may differ from a plain program's by a relative error of at most 0.0055.
Values may be sent and summed in bfloat16 or wider, within the bound.
A program may use at most 64 MiB of HBM per device.

v0:
```python
import jax
import jax.numpy as jnp
from jax import lax
from jax.sharding import PartitionSpec as P

FIRST_DILATION = 4
SECOND_DILATION = 8


def padded(array, sides, width):
    for axis, dim in sides:
        peers, length = (lax.axis_size(axis), array.shape[dim])
        up = [(i, (i + 1) % peers) for i in range(peers - 1)]
        down = [(j, i) for i, j in up]
        last = lax.slice_in_dim(array, length - width, length, axis=dim)
        leading = lax.slice_in_dim(array, 0, width, axis=dim)
        before = lax.ppermute(last, axis, up)
        after = lax.ppermute(leading, axis, down)
        array = jnp.concatenate([before, array, after], axis=dim)
    return array


def swapped(value, axis, bit):
    mask = 2**bit
    pairs = [(source, source ^ mask) for source in range(lax.axis_size(axis))]
    return lax.ppermute(value, axis, pairs)


def dilated_conv(active, weight, spacing, out_rows, out_cols):
    windows = []
    for tap_row in range(3):
        for tap_col in range(3):
            windows.append(
                active[
                    tap_row * spacing : tap_row * spacing + out_rows,
                    tap_col * spacing : tap_col * spacing + out_cols,
                ]
            )
    stacked = jnp.concatenate(windows, axis=-1)
    flat_weight = weight.reshape(9 * weight.shape[2], weight.shape[3])
    return jnp.einsum("rch,hk->rck", stacked, flat_weight, preferred_element_type=jnp.float32)


def on_device(
    map_in,
    embedding,
    w_row,
    w_col,
    first_kernel_weight,
    first_bias,
    second_kernel_weight,
    second_bias,
    w_mix,
    b_mix,
    w_head,
):
    patch_rows, patch_columns, channels = map_in.shape
    row_count = lax.axis_size("row")
    row_at = lax.axis_index("row")
    col_at = lax.axis_index("col")
    all_bins = lax.all_gather(embedding, "row", axis=0, tiled=True)
    row_terms = jnp.dot(all_bins, w_row, preferred_element_type=jnp.float32)
    col_terms = jnp.dot(all_bins, w_col, preferred_element_type=jnp.float32)
    own_rows = lax.dynamic_slice_in_dim(row_terms, row_at * patch_rows, patch_rows, 0)
    own_cols = lax.dynamic_slice_in_dim(col_terms, col_at * patch_columns, patch_columns, 0)
    contact_grid = (
        map_in.astype(jnp.float32) + own_rows[:, None, :] + own_cols[None, :, :]
    ).astype(jnp.bfloat16)
    first_padded = padded(contact_grid, (("row", 0), ("col", 1)), FIRST_DILATION)
    first_layer = (
        contact_grid.astype(jnp.float32)
        + dilated_conv(
            jnp.maximum(first_padded, 0),
            first_kernel_weight,
            FIRST_DILATION,
            patch_rows,
            patch_columns,
        )
        + first_bias
    ).astype(jnp.bfloat16)
    second_padded = padded(first_layer, (("row", 0), ("col", 1)), SECOND_DILATION)
    second_layer = (
        first_layer.astype(jnp.float32)
        + dilated_conv(
            jnp.maximum(second_padded, 0),
            second_kernel_weight,
            SECOND_DILATION,
            patch_rows,
            patch_columns,
        )
        + second_bias
    ).astype(jnp.bfloat16)
    half_rows = patch_rows // 2
    blocks_per = row_count // 2
    arranged = second_layer.reshape(2, half_rows, blocks_per, patch_rows, channels)
    arranged = arranged.transpose(0, 2, 1, 3, 4).reshape(
        2 * blocks_per, half_rows, patch_rows, channels
    )
    exchanged = lax.all_to_all(
        lax.all_to_all(arranged, "row", split_axis=0, concat_axis=0, tiled=True),
        "col",
        split_axis=0,
        concat_axis=0,
        tiled=True,
    )
    exchanged = exchanged.reshape(2, blocks_per, half_rows, patch_rows, channels)
    top_half = row_at // blocks_per
    kept_part = lax.dynamic_index_in_dim(exchanged, top_half, 0, keepdims=False)
    sent_part = lax.dynamic_index_in_dim(exchanged, 1 - top_half, 0, keepdims=False)
    came_back = swapped(sent_part, "row", blocks_per.bit_length() - 1)
    stacked = jnp.where(
        top_half == 0, jnp.stack([kept_part, came_back]), jnp.stack([came_back, kept_part])
    )
    mirrored = stacked.transpose(3, 1, 0, 2, 4).reshape(patch_rows, patch_columns, channels)
    symmetric = ((second_layer.astype(jnp.float32) + mirrored.astype(jnp.float32)) * 0.5).astype(
        jnp.bfloat16
    )
    mixture = (
        jnp.einsum("rch,hk->rck", symmetric, w_mix, preferred_element_type=jnp.float32) + b_mix
    )
    mixture = jnp.maximum(mixture, 0.0)
    return jnp.sum(mixture * w_head, axis=-1)


def solution(mesh):
    placed = (
        P(("group", "row"), "col", None),
        P(("group", "row"), None),
        P(),
        P(),
        P(),
        P(),
        P(),
        P(),
        P(),
        P(),
        P(),
    )
    return jax.shard_map(
        on_device, mesh=mesh, in_specs=placed, out_specs=P(("group", "row"), "col"), check_vma=False
    )
```

profile of v0, /device:TPU:0, one launch (start us, length us, event | category | flops | bytes accessed | tf_op | source)
XLA Modules:
  0.0 92.6 jit_solution(15328792908924847365)
XLA Ops:
  0.0 0.7 copy-done.5
  0.7 32.3 %all-gather = bf16[8,12,96]{2,1,0:T(8,128)(2,1)S(1)} all-gather(bf16[1,12,96]{2,1,0:T(8,128)(2,1)S(1)} %bitcast.32), channel_id=1, replica_groups=mesh['group'=2,'row'=8,'col'=2] {'row'}, dimensions={0}, use_global_device_ids=true | all-gather | bytes 20736 | tf_op jit(solution)/shard_map/all_gather | solution.py:61
  33.1 0.1 fusion.14
  33.2 0.1 fusion.15
  33.4 0.6 copy-done.1
  34.0 3.4 %collective-permute-start = (bf16[4,48,48]{2,1,0:T(8,128)(2,1)S(1)}, bf16[4,48,48]{2,1,0:T(8,128)(2,1)S(1)}, u32[]{:S(2)}, u32[]{:S(2)}) collective-permute-start(bf16[4,48,48]{2,1,0:T(8,128)(2,1)S(1)} %get-tuple-element.31), channel_id=1, source_target_pairs={{0,2},{2,4},{4,6},{6,8},{8,10},{10,12},{12,14},{1,3},{3,5},{5,7},{... | collective-permute-start | bytes 55304 | tf_op jit(solution)/shard_map/ppermute | solution.py:17
  37.4 1.3 %collective-permute-start.1 = (bf16[4,48,48]{2,1,0:T(8,128)(2,1)S(1)}, bf16[4,48,48]{2,1,0:T(8,128)(2,1)S(1)}, u32[]{:S(2)}, u32[]{:S(2)}) collective-permute-start(bf16[4,48,48]{2,1,0:T(8,128)(2,1)S(1)} %get-tuple-element.32), channel_id=1, source_target_pairs={{2,0},{4,2},{6,4},{8,6},{10,8},{12,10},{14,12},{3,1},{5,3},{7,5},{... | collective-permute-start | bytes 55304 | tf_op jit(solution)/shard_map/ppermute | solution.py:18
  38.7 0.4 collective-permute-done
  39.2 4.3 %collective-permute-done.1 = bf16[4,48,48]{2,1,0:T(8,128)(2,1)S(1)} collective-permute-done((bf16[4,48,48]{2,1,0:T(8,128)(2,1)S(1)}, bf16[4,48,48]{2,1,0:T(8,128)(2,1)S(1)}, u32[]{:S(2)}, u32[]{:S(2)}) %collective-permute-start.1) | collective-permute-done | bytes 18464 | tf_op jit(solution)/shard_map/ppermute | solution.py:18
  43.4 1.3 %collective-permute-start.2 = (bf16[20,4,48]{2,1,0:T(4,128)(2,1)S(1)}, bf16[20,4,48]{2,1,0:T(4,128)(2,1)S(1)}, u32[]{:S(2)}, u32[]{:S(2)}) collective-permute-start(bf16[20,4,48]{2,1,0:T(4,128)(2,1)S(1)} %get-tuple-element.25), channel_id=1, source_target_pairs={{0,1},{2,3},{4,5},{6,7},{8,9},{10,11},{12,13},{14,15},{16,17},{18,... | collective-permute-start | bytes 23048 | tf_op jit(solution)/shard_map/ppermute | solution.py:17
  44.7 1.3 %collective-permute-start.3 = (bf16[20,4,48]{2,1,0:T(4,128)(2,1)S(1)}, bf16[20,4,48]{2,1,0:T(4,128)(2,1)S(1)}, u32[]{:S(2)}, u32[]{:S(2)}) collective-permute-start(bf16[20,4,48]{2,1,0:T(4,128)(2,1)S(1)} %get-tuple-element.26), channel_id=1, source_target_pairs={{1,0},{3,2},{5,4},{7,6},{9,8},{11,10},{13,12},{15,14},{17,16},{19,... | collective-permute-start | bytes 23048 | tf_op jit(solution)/shard_map/ppermute | solution.py:18
  46.0 1.8 %collective-permute-done.3 = bf16[20,4,48]{2,1,0:T(4,128)(2,1)S(1)} collective-permute-done((bf16[20,4,48]{2,1,0:T(4,128)(2,1)S(1)}, bf16[20,4,48]{2,1,0:T(4,128)(2,1)S(1)}, u32[]{:S(2)}, u32[]{:S(2)}) %collective-permute-start.3) | collective-permute-done | bytes 7712 | tf_op jit(solution)/shard_map/ppermute | solution.py:18
  47.8 0.1 maximum_maximum_fusion.1
  48.0 0.2 fusion.11
  48.2 0.6 concatenate.20
  48.8 0.6 copy-done.6
  49.5 0.3 fusion.5
  49.8 2.8 %collective-permute-start.4 = (bf16[8,48,48]{2,1,0:T(8,128)(2,1)S(1)}, bf16[8,48,48]{2,1,0:T(8,128)(2,1)S(1)}, u32[]{:S(2)}, u32[]{:S(2)}) collective-permute-start(bf16[8,48,48]{2,1,0:T(8,128)(2,1)S(1)} %get-tuple-element.29), channel_id=1, source_target_pairs={{0,2},{2,4},{4,6},{6,8},{8,10},{10,12},{12,14},{1,3},{3,5},{5,7},{... | collective-permute-start | bytes 110600 | tf_op jit(solution)/shard_map/ppermute | solution.py:17
  52.7 1.3 %collective-permute-start.5 = (bf16[8,48,48]{2,1,0:T(8,128)(2,1)S(1)}, bf16[8,48,48]{2,1,0:T(8,128)(2,1)S(1)}, u32[]{:S(2)}, u32[]{:S(2)}) collective-permute-start(bf16[8,48,48]{2,1,0:T(8,128)(2,1)S(1)} %get-tuple-element.30), channel_id=1, source_target_pairs={{2,0},{4,2},{6,4},{8,6},{10,8},{12,10},{14,12},{3,1},{5,3},{7,5},{... | collective-permute-start | bytes 110600 | tf_op jit(solution)/shard_map/ppermute | solution.py:18
  54.0 1.1 %collective-permute-done.4 = bf16[8,48,48]{2,1,0:T(8,128)(2,1)S(1)} collective-permute-done((bf16[8,48,48]{2,1,0:T(8,128)(2,1)S(1)}, bf16[8,48,48]{2,1,0:T(8,128)(2,1)S(1)}, u32[]{:S(2)}, u32[]{:S(2)}) %collective-permute-start.4) | collective-permute-done | bytes 36896 | tf_op jit(solution)/shard_map/ppermute | solution.py:17
  55.0 4.2 %collective-permute-done.5 = bf16[8,48,48]{2,1,0:T(8,128)(2,1)S(1)} collective-permute-done((bf16[8,48,48]{2,1,0:T(8,128)(2,1)S(1)}, bf16[8,48,48]{2,1,0:T(8,128)(2,1)S(1)}, u32[]{:S(2)}, u32[]{:S(2)}) %collective-permute-start.5) | collective-permute-done | bytes 36896 | tf_op jit(solution)/shard_map/ppermute | solution.py:18
  59.2 1.3 %collective-permute-start.6 = (bf16[28,8,48]{2,1,0:T(8,128)(2,1)S(1)}, bf16[28,8,48]{2,1,0:T(8,128)(2,1)S(1)}, u32[]{:S(2)}, u32[]{:S(2)}) collective-permute-start(bf16[28,8,48]{2,1,0:T(8,128)(2,1)S(1)} %get-tuple-element.14), channel_id=1, source_target_pairs={{0,1},{2,3},{4,5},{6,7},{8,9},{10,11},{12,13},{14,15},{16,17},{18,... | collective-permute-start | bytes 64520 | tf_op jit(solution)/shard_map/ppermute | solution.py:17
  60.5 1.3 %collective-permute-start.7 = (bf16[28,8,48]{2,1,0:T(8,128)(2,1)S(1)}, bf16[28,8,48]{2,1,0:T(8,128)(2,1)S(1)}, u32[]{:S(2)}, u32[]{:S(2)}) collective-permute-start(bf16[28,8,48]{2,1,0:T(8,128)(2,1)S(1)} %get-tuple-element.15), channel_id=1, source_target_pairs={{1,0},{3,2},{5,4},{7,6},{9,8},{11,10},{13,12},{15,14},{17,16},{19,... | collective-permute-start | bytes 64520 | tf_op jit(solution)/shard_map/ppermute | solution.py:18
  61.8 1.8 %collective-permute-done.7 = bf16[28,8,48]{2,1,0:T(8,128)(2,1)S(1)} collective-permute-done((bf16[28,8,48]{2,1,0:T(8,128)(2,1)S(1)}, bf16[28,8,48]{2,1,0:T(8,128)(2,1)S(1)}, u32[]{:S(2)}, u32[]{:S(2)}) %collective-permute-start.7) | collective-permute-done | bytes 21536 | tf_op jit(solution)/shard_map/ppermute | solution.py:18
  63.6 0.1 maximum_maximum_fusion
  63.8 0.2 fusion.10
  64.0 0.0 copy-start.2
  64.0 0.6 concatenate.23
  64.6 0.2 copy-done.2
  64.9 0.4 copy-done.7
  65.3 0.3 fusion.4
  65.6 0.1 reshape.26
  65.7 0.1 copy.22
  65.8 0.8 reshape.35
  66.6 6.0 %all-to-all-start = ((bf16[8,2,1728]{2,1,0:T(2,128)(2,1)}), bf16[8,2,1728]{2,1,0:T(2,128)(2,1)S(1)}, u32[]{:S(2)}, u32[]{:S(2)}) async-start(bf16[8,2,1728]{2,1,0:T(2,128)(2,1)} %reshape.35), calls=%async_computation | async-start | bytes 114688 | tf_op jit(solution)/shard_map/all_to_all | solution.py:100
  72.6 6.8 %all-to-all-done = bf16[8,2,1728]{2,1,0:T(2,128)(2,1)S(1)} async-done(((bf16[8,2,1728]{2,1,0:T(2,128)(2,1)}), bf16[8,2,1728]{2,1,0:T(2,128)(2,1)S(1)}, u32[]{:S(2)}, u32[]{:S(2)}) %all-to-all-start) | async-done | bytes 55328 | tf_op jit(solution)/shard_map/all_to_all | solution.py:100
  79.4 0.2 reshape.36
  79.7 0.2 reshape.37
  79.9 3.8 %all_to_all.10 = bf16[2,2,6912]{2,1,0:T(2,128)(2,1)S(1)} all-to-all(bf16[2,2,6912]{2,1,0:T(2,128)(2,1)S(1)} %reshape.37), channel_id=1, replica_groups=mesh['group'=2,'row'=8,'col'=2] {'col'}, dimensions={0} | all-to-all | bytes 110592 | tf_op jit(solution)/shard_map/all_to_all | solution.py:99
  83.7 0.2 reshape.38
  83.9 0.1 copy.24
  84.0 0.1 constant_dynamic-slice_fusion
  84.1 0.6 collective-permute-start.8
  84.6 6.0 %collective-permute-done.8 = bf16[4,6,12,48]{3,0,2,1:T(4,128)(2,1)S(1)} collective-permute-done((bf16[4,6,12,48]{3,0,2,1:T(4,128)(2,1)S(1)}, bf16[4,6,12,48]{3,0,2,1:T(4,128)(2,1)S(1)}, u32[]{:S(2)}, u32[]{:S(2)}) %collective-permute-start.8) | collective-permute-done | bytes 27680 | tf_op jit(solution)/shard_map/ppermute | solution.py:26
  90.7 0.2 convert_bitcast_fusion
  90.8 0.2 copy.25
  91.1 0.6 copy-done.8
  91.7 0.9 fusion.6
  (27 shorter events, 0.3 us)
Async XLA Ops:
  0.0 48.8 %copy-start = (bf16[3,3,48,48]{3,2,1,0:T(8,128)(2,1)S(1)}, bf16[3,3,48,48]{3,2,1,0:T(8,128)(2,1)}, u32[]{:S(2)}) copy-start(bf16[3,3,48,48]{3,2,1,0:T(8,128)(2,1)} %param.15) | copy-start | bytes 124420
  0.0 0.7 copy-start.5
  0.7 32.3 %copy-start.3 = (bf16[96,48]{0,1:T(8,128)(2,1)S(1)}, bf16[96,48]{0,1:T(8,128)(2,1)}, u32[]{:S(2)}) copy-start(bf16[96,48]{0,1:T(8,128)(2,1)} %param.13) | copy-start | bytes 27652
  0.7 32.5 %copy-start.4 = (bf16[96,48]{0,1:T(8,128)(2,1)S(1)}, bf16[96,48]{0,1:T(8,128)(2,1)}, u32[]{:S(2)}) copy-start(bf16[96,48]{0,1:T(8,128)(2,1)} %param.14) | copy-start | bytes 27652
  33.0 0.9 copy-start.1
  34.0 5.1 %collective-permute-start = (bf16[4,48,48]{2,1,0:T(8,128)(2,1)S(1)}, bf16[4,48,48]{2,1,0:T(8,128)(2,1)S(1)}, u32[]{:S(2)}, u32[]{:S(2)}) collective-permute-start(bf16[4,48,48]{2,1,0:T(8,128)(2,1)S(1)} %get-tuple-element.31), channel_id=1, source_target_pairs={{0,2},{2,4},{4,6},{6,8},{8,10},{10,12},{12,14},{1,3},{3,5},{5,7},{... | collective-permute-start | bytes 55304 | tf_op jit(solution)/shard_map/ppermute | solution.py:17
  37.4 6.0 %collective-permute-start.1 = (bf16[4,48,48]{2,1,0:T(8,128)(2,1)S(1)}, bf16[4,48,48]{2,1,0:T(8,128)(2,1)S(1)}, u32[]{:S(2)}, u32[]{:S(2)}) collective-permute-start(bf16[4,48,48]{2,1,0:T(8,128)(2,1)S(1)} %get-tuple-element.32), channel_id=1, source_target_pairs={{2,0},{4,2},{6,4},{8,6},{10,8},{12,10},{14,12},{3,1},{5,3},{7,5},{... | collective-permute-start | bytes 55304 | tf_op jit(solution)/shard_map/ppermute | solution.py:18
  43.4 2.6 %collective-permute-start.2 = (bf16[20,4,48]{2,1,0:T(4,128)(2,1)S(1)}, bf16[20,4,48]{2,1,0:T(4,128)(2,1)S(1)}, u32[]{:S(2)}, u32[]{:S(2)}) collective-permute-start(bf16[20,4,48]{2,1,0:T(4,128)(2,1)S(1)} %get-tuple-element.25), channel_id=1, source_target_pairs={{0,1},{2,3},{4,5},{6,7},{8,9},{10,11},{12,13},{14,15},{16,17},{18,... | collective-permute-start | bytes 23048 | tf_op jit(solution)/shard_map/ppermute | solution.py:17
  44.7 3.1 %collective-permute-start.3 = (bf16[20,4,48]{2,1,0:T(4,128)(2,1)S(1)}, bf16[20,4,48]{2,1,0:T(4,128)(2,1)S(1)}, u32[]{:S(2)}, u32[]{:S(2)}) collective-permute-start(bf16[20,4,48]{2,1,0:T(4,128)(2,1)S(1)} %get-tuple-element.26), channel_id=1, source_target_pairs={{1,0},{3,2},{5,4},{7,6},{9,8},{11,10},{13,12},{15,14},{17,16},{19,... | collective-permute-start | bytes 23048 | tf_op jit(solution)/shard_map/ppermute | solution.py:18
  48.8 0.7 copy-start.6
  49.8 5.2 %collective-permute-start.4 = (bf16[8,48,48]{2,1,0:T(8,128)(2,1)S(1)}, bf16[8,48,48]{2,1,0:T(8,128)(2,1)S(1)}, u32[]{:S(2)}, u32[]{:S(2)}) collective-permute-start(bf16[8,48,48]{2,1,0:T(8,128)(2,1)S(1)} %get-tuple-element.29), channel_id=1, source_target_pairs={{0,2},{2,4},{4,6},{6,8},{8,10},{10,12},{12,14},{1,3},{3,5},{5,7},{... | collective-permute-start | bytes 110600 | tf_op jit(solution)/shard_map/ppermute | solution.py:17
  52.7 6.5 %collective-permute-start.5 = (bf16[8,48,48]{2,1,0:T(8,128)(2,1)S(1)}, bf16[8,48,48]{2,1,0:T(8,128)(2,1)S(1)}, u32[]{:S(2)}, u32[]{:S(2)}) collective-permute-start(bf16[8,48,48]{2,1,0:T(8,128)(2,1)S(1)} %get-tuple-element.30), channel_id=1, source_target_pairs={{2,0},{4,2},{6,4},{8,6},{10,8},{12,10},{14,12},{3,1},{5,3},{7,5},{... | collective-permute-start | bytes 110600 | tf_op jit(solution)/shard_map/ppermute | solution.py:18
  59.2 2.6 %collective-permute-start.6 = (bf16[28,8,48]{2,1,0:T(8,128)(2,1)S(1)}, bf16[28,8,48]{2,1,0:T(8,128)(2,1)S(1)}, u32[]{:S(2)}, u32[]{:S(2)}) collective-permute-start(bf16[28,8,48]{2,1,0:T(8,128)(2,1)S(1)} %get-tuple-element.14), channel_id=1, source_target_pairs={{0,1},{2,3},{4,5},{6,7},{8,9},{10,11},{12,13},{14,15},{16,17},{18,... | collective-permute-start | bytes 64520 | tf_op jit(solution)/shard_map/ppermute | solution.py:17
  60.5 3.1 %collective-permute-start.7 = (bf16[28,8,48]{2,1,0:T(8,128)(2,1)S(1)}, bf16[28,8,48]{2,1,0:T(8,128)(2,1)S(1)}, u32[]{:S(2)}, u32[]{:S(2)}) collective-permute-start(bf16[28,8,48]{2,1,0:T(8,128)(2,1)S(1)} %get-tuple-element.15), channel_id=1, source_target_pairs={{1,0},{3,2},{5,4},{7,6},{9,8},{11,10},{13,12},{15,14},{17,16},{19,... | collective-permute-start | bytes 64520 | tf_op jit(solution)/shard_map/ppermute | solution.py:18
  64.0 0.9 copy-start.2
  64.6 0.7 copy-start.7
  66.6 12.8 %all-to-all-start = ((bf16[8,2,1728]{2,1,0:T(2,128)(2,1)}), bf16[8,2,1728]{2,1,0:T(2,128)(2,1)S(1)}, u32[]{:S(2)}, u32[]{:S(2)}) async-start(bf16[8,2,1728]{2,1,0:T(2,128)(2,1)} %reshape.35), calls=%async_computation | async-start | bytes 114688 | tf_op jit(solution)/shard_map/all_to_all | solution.py:100
  84.1 6.6 %collective-permute-start.8 = (bf16[4,6,12,48]{3,0,2,1:T(4,128)(2,1)S(1)}, bf16[4,6,12,48]{3,0,2,1:T(4,128)(2,1)S(1)}, u32[]{:S(2)}, u32[]{:S(2)}) collective-permute-start(bf16[4,6,12,48]{3,0,2,1:T(4,128)(2,1)S(1)} %get-tuple-element.28), channel_id=1, source_target_pairs={{0,8},{2,10},{4,12},{6,14},{8,0},{10,2},{12,4},{14,6},{1,9},{3,11}... | collective-permute-start | bytes 82952 | tf_op jit(solution)/shard_map/ppermute | solution.py:26
  91.0 0.7 copy-start.8
  91.0 0.7 copy-start.9
  91.0 0.7 copy-start.10
where the time goes:
time: 93.2 us; the launch traced here: 92.6 us
  blocking collectives  36.1 us (39%)
  waiting for transfers between devices  26.4 us (28%)
  starting transfers between devices  20.5 us (22%)
  local copies, waits for them, and re-layouts  7.02 us (8%)
  matrix products  1.8 us (2%)
    all_gather x1, blocking collectives, on_device(): all_bins = lax.all_gather(embedding, 'row', axis=0, tiled=True)  32.3 us
    ppermute x4, waiting for transfers between devices, padded(): after = lax.ppermute(leading, axis, down)  12 us
    ppermute x4, starting transfers between devices, padded(): before = lax.ppermute(last, axis, up)  8.8 us
    all_to_all x1, waiting for transfers between devices, on_device(): lax.all_to_all(arranged, 'row', split_axis=0, concat_axis=0, tiled=True)  6.85 us
    ppermute x1, waiting for transfers between devices, swapped(): return lax.ppermute(value, axis, pairs)  6.02 us
    all_to_all x1, starting transfers between devices, on_device(): lax.all_to_all(arranged, 'row', split_axis=0, concat_axis=0, tiled=True)  5.98 us
    ppermute x4, starting transfers between devices, padded(): after = lax.ppermute(leading, axis, down)  5.17 us
    unnamed x27, local copies, waits for them, and re-layouts  4.82 us
  transfers between devices with their start and end apart: 10, of which 8 were waited for; matrix products, arithmetic and copies ran while one was open for 0% of the time, Pallas kernels for 0%

commit v1 on v0

--- a/solution.py
+++ b/solution.py
@@ -2,9 +2,17 @@
 import jax.numpy as jnp
 from jax import lax
 from jax.sharding import PartitionSpec as P
+from jax.lax import axis_index, axis_size, ppermute
 
 FIRST_DILATION = 4
 SECOND_DILATION = 8
+
+
+def extend_the_ranges(frame_in, which_dim):
+    row_out = list(frame_in.shape[1:])
+    row_out[which_dim] *= frame_in.shape[0]
+    moved = jnp.moveaxis(frame_in, 0, which_dim).reshape(row_out)
+    return moved
 
 
 def padded(array, sides, width):
@@ -58,7 +66,21 @@
     row_count = lax.axis_size("row")
     row_at = lax.axis_index("row")
     col_at = lax.axis_index("col")
-    all_bins = lax.all_gather(embedding, "row", axis=0, tiled=True)
+    wide_n = axis_size("row")
+    panels = [(ix, (ix + 1) % wide_n) for ix in range(wide_n)]
+    store = [(it, src_i) for src_i, it in panels]
+    s_next, even = ([], [])
+    for s in range(wide_n - 1):
+        if s % 2 == 0:
+            s_next.append(
+                ppermute(s_next[-1] if s_next else embedding, axis_name="row", perm=panels)
+            )
+        else:
+            even.append(ppermute(even[-1] if even else embedding, "row", store))
+    u1 = jnp.stack([*s_next[::-1], embedding, *even], axis=0)
+    lower = axis_index("row") - len(s_next)
+    u1 = u1[(jnp.arange(wide_n) - lower) % wide_n]
+    all_bins = extend_the_ranges(u1, 0)
     row_terms = jnp.dot(all_bins, w_row, preferred_element_type=jnp.float32)
     col_terms = jnp.dot(all_bins, w_col, preferred_element_type=jnp.float32)
     own_rows = lax.dynamic_slice_in_dim(row_terms, row_at * patch_rows, patch_rows, 0)

time: 93.2 us -> 89.2 us (0.957)
  blocking collectives: 36.1 us -> 3.77 us
  starting transfers between devices: 20.5 us -> 39.7 us
  waiting for transfers between devices: 26.4 us -> 34.7 us
    all_gather x1 -> x0, blocking collectives: 32.3 us -> none  [on_device(): all_bins = lax.all_gather(embedding, 'row', axis=0, tiled=True)]
    ppermute x0 -> x7, starting transfers between devices: none -> 17.5 us  [the longest x3 14.5 us: on_device(): even.append(ppermute(even[-1] if even else embedding, 'row', store))]
    ppermute x0 -> x7, waiting for transfers between devices: none -> 9.16 us  [the longest x4 9.15 us: on_device(): ppermute(s_next[-1] if s_next else embedding, axis_name='row', perm=panels)]
    all_to_all x1, starting transfers between devices: 5.98 us -> 9.31 us  [on_device(): lax.all_to_all(arranged, 'row', split_axis=0, concat_axis=0, tiled=True)]
    ppermute x4, waiting for transfers between devices: 12 us -> 10.2 us  [padded(): after = lax.ppermute(leading, axis, down)]
    ppermute x4, starting transfers between devices: 8.8 us -> 7.21 us  [padded(): before = lax.ppermute(last, axis, up)]
    ppermute x4, waiting for transfers between devices: 1.5 us -> 2.49 us  [padded(): before = lax.ppermute(last, axis, up)]
    unnamed x27 -> x33, local copies, waits for them, and re-layouts: 4.82 us -> 4.82 us
  transfers between devices with their start and end apart: 10 -> 17, of which waited for: 8 -> 12; matrix products, arithmetic and copies ran while one was open for 0% -> 0% of each run, Pallas kernels for 0% -> 0%
where the time goes in v1:
time: 89.2 us; the launch traced here: 88.5 us
  starting transfers between devices  39.7 us (45%)
  waiting for transfers between devices  34.7 us (39%)
  local copies, waits for them, and re-layouts  7.61 us (9%)
  blocking collectives  3.77 us (4%)
  matrix products  1.8 us (2%)
    ppermute x3, starting transfers between devices, on_device(): even.append(ppermute(even[-1] if even else embedding, 'row', store))  14.5 us
    ppermute x4, waiting for transfers between devices, padded(): after = lax.ppermute(leading, axis, down)  10.2 us
    all_to_all x1, starting transfers between devices, on_device(): lax.all_to_all(arranged, 'row', split_axis=0, concat_axis=0, tiled=True)  9.31 us
    ppermute x4, waiting for transfers between devices, on_device(): ppermute(s_next[-1] if s_next else embedding, axis_name='row', perm=panels)  9.15 us
    ppermute x4, starting transfers between devices, padded(): before = lax.ppermute(last, axis, up)  7.21 us
    all_to_all x1, waiting for transfers between devices, on_device(): lax.all_to_all(arranged, 'row', split_axis=0, concat_axis=0, tiled=True)  6.85 us
    ppermute x1, waiting for transfers between devices, swapped(): return lax.ppermute(value, axis, pairs)  6.02 us
    ppermute x4, starting transfers between devices, padded(): after = lax.ppermute(leading, axis, down)  5.17 us
  transfers between devices with their start and end apart: 17, of which 12 were waited for; matrix products, arithmetic and copies ran while one was open for 0% of the time, Pallas kernels for 0%

profile of v1, /device:TPU:0, one launch (start us, length us, event | category | flops | bytes accessed | tf_op | source)
XLA Modules:
  0.0 88.5 jit_solution(2456109189478514759)
XLA Ops:
  0.0 2.9 %collective-permute-start = (bf16[12,96]{1,0:T(8,128)(2,1)}, bf16[12,96]{1,0:T(8,128)(2,1)S(1)}, u32[]{:S(2)}, u32[]{:S(2)}) collective-permute-start(bf16[12,96]{1,0:T(8,128)(2,1)} %param.12), channel_id=1, source_target_pairs={{0,2},{2,4},{4,6},{6,8},{8,10},{10,12},{12,14},{14,0},{1,3},{3,5},... | collective-permute-start | bytes 6920 | tf_op jit(solution)/shard_map/ppermute | solution.py:76
  2.9 4.8 %collective-permute-done = bf16[12,96]{1,0:T(8,128)(2,1)S(1)} collective-permute-done((bf16[12,96]{1,0:T(8,128)(2,1)}, bf16[12,96]{1,0:T(8,128)(2,1)S(1)}, u32[]{:S(2)}, u32[]{:S(2)}) %collective-permute-start) | collective-permute-done | bytes 2336 | tf_op jit(solution)/shard_map/ppermute | solution.py:76
  7.8 4.7 %collective-permute-start.4 = (bf16[12,96]{1,0:T(8,128)(2,1)}, bf16[12,96]{1,0:T(8,128)(2,1)S(1)}, u32[]{:S(2)}, u32[]{:S(2)}) collective-permute-start(bf16[12,96]{1,0:T(8,128)(2,1)} %param.12), channel_id=1, source_target_pairs={{2,0},{4,2},{6,4},{8,6},{10,8},{12,10},{14,12},{0,14},{3,1},{5,3},... | collective-permute-start | bytes 6920 | tf_op jit(solution)/shard_map/ppermute | solution.py:79
  12.5 1.6 %collective-permute-done.1 = bf16[12,96]{1,0:T(8,128)(2,1)S(1)} collective-permute-done((bf16[12,96]{1,0:T(8,128)(2,1)S(1)}, bf16[12,96]{1,0:T(8,128)(2,1)S(1)}, u32[]{:S(2)}, u32[]{:S(2)}) %collective-permute-start.1) | collective-permute-done | bytes 2336 | tf_op jit(solution)/shard_map/ppermute | solution.py:76
  14.1 4.9 %collective-permute-start.5 = (bf16[12,96]{1,0:T(8,128)(2,1)S(1)}, bf16[12,96]{1,0:T(8,128)(2,1)S(1)}, u32[]{:S(2)}, u32[]{:S(2)}) collective-permute-start(bf16[12,96]{1,0:T(8,128)(2,1)S(1)} %collective-permute-done.4), channel_id=1, source_target_pairs={{2,0},{4,2},{6,4},{8,6},{10,8},{12,10},{14,12},{0,14},{3,1},{5,3},... | collective-permute-start | bytes 6920 | tf_op jit(solution)/shard_map/ppermute | solution.py:79
  19.0 1.4 %collective-permute-done.2 = bf16[12,96]{1,0:T(8,128)(2,1)S(1)} collective-permute-done((bf16[12,96]{1,0:T(8,128)(2,1)S(1)}, bf16[12,96]{1,0:T(8,128)(2,1)S(1)}, u32[]{:S(2)}, u32[]{:S(2)}) %collective-permute-start.2) | collective-permute-done | bytes 2336 | tf_op jit(solution)/shard_map/ppermute | solution.py:76
  20.4 4.9 %collective-permute-start.6 = (bf16[12,96]{1,0:T(8,128)(2,1)S(1)}, bf16[12,96]{1,0:T(8,128)(2,1)S(1)}, u32[]{:S(2)}, u32[]{:S(2)}) collective-permute-start(bf16[12,96]{1,0:T(8,128)(2,1)S(1)} %collective-permute-done.5), channel_id=1, source_target_pairs={{2,0},{4,2},{6,4},{8,6},{10,8},{12,10},{14,12},{0,14},{3,1},{5,3},... | collective-permute-start | bytes 6920 | tf_op jit(solution)/shard_map/ppermute | solution.py:79
  25.3 1.4 %collective-permute-done.3 = bf16[12,96]{1,0:T(8,128)(2,1)S(1)} collective-permute-done((bf16[12,96]{1,0:T(8,128)(2,1)S(1)}, bf16[12,96]{1,0:T(8,128)(2,1)S(1)}, u32[]{:S(2)}, u32[]{:S(2)}) %collective-permute-start.3) | collective-permute-done | bytes 2336 | tf_op jit(solution)/shard_map/ppermute | solution.py:76
  26.7 0.7 copy-done.5
  27.5 0.6 gather_fusion
  28.4 0.5 copy-done.1
  29.0 1.3 %collective-permute-start.7 = (bf16[4,48,48]{2,1,0:T(8,128)(2,1)S(1)}, bf16[4,48,48]{2,1,0:T(8,128)(2,1)S(1)}, u32[]{:S(2)}, u32[]{:S(2)}) collective-permute-start(bf16[4,48,48]{2,1,0:T(8,128)(2,1)S(1)} %get-tuple-element.31), channel_id=1, source_target_pairs={{0,2},{2,4},{4,6},{6,8},{8,10},{10,12},{12,14},{1,3},{3,5},{5,7},{... | collective-permute-start | bytes 55304 | tf_op jit(solution)/shard_map/ppermute | solution.py:25
  30.3 1.3 %collective-permute-start.8 = (bf16[4,48,48]{2,1,0:T(8,128)(2,1)S(1)}, bf16[4,48,48]{2,1,0:T(8,128)(2,1)S(1)}, u32[]{:S(2)}, u32[]{:S(2)}) collective-permute-start(bf16[4,48,48]{2,1,0:T(8,128)(2,1)S(1)} %get-tuple-element.32), channel_id=1, source_target_pairs={{2,0},{4,2},{6,4},{8,6},{10,8},{12,10},{14,12},{3,1},{5,3},{7,5},{... | collective-permute-start | bytes 55304 | tf_op jit(solution)/shard_map/ppermute | solution.py:26
  31.6 0.4 collective-permute-done.7
  32.0 4.3 %collective-permute-done.8 = bf16[4,48,48]{2,1,0:T(8,128)(2,1)S(1)} collective-permute-done((bf16[4,48,48]{2,1,0:T(8,128)(2,1)S(1)}, bf16[4,48,48]{2,1,0:T(8,128)(2,1)S(1)}, u32[]{:S(2)}, u32[]{:S(2)}) %collective-permute-start.8) | collective-permute-done | bytes 18464 | tf_op jit(solution)/shard_map/ppermute | solution.py:26
  36.3 1.3 %collective-permute-start.10 = (bf16[20,4,48]{2,1,0:T(4,128)(2,1)S(1)}, bf16[20,4,48]{2,1,0:T(4,128)(2,1)S(1)}, u32[]{:S(2)}, u32[]{:S(2)}) collective-permute-start(bf16[20,4,48]{2,1,0:T(4,128)(2,1)S(1)} %get-tuple-element.26), channel_id=1, source_target_pairs={{1,0},{3,2},{5,4},{7,6},{9,8},{11,10},{13,12},{15,14},{17,16},{19,... | collective-permute-start | bytes 23048 | tf_op jit(solution)/shard_map/ppermute | solution.py:26
  37.6 3.0 %collective-permute-start.9 = (bf16[20,4,48]{2,1,0:T(4,128)(2,1)S(1)}, bf16[20,4,48]{2,1,0:T(4,128)(2,1)S(1)}, u32[]{:S(2)}, u32[]{:S(2)}) collective-permute-start(bf16[20,4,48]{2,1,0:T(4,128)(2,1)S(1)} %get-tuple-element.25), channel_id=1, source_target_pairs={{0,1},{2,3},{4,5},{6,7},{8,9},{10,11},{12,13},{14,15},{16,17},{18,... | collective-permute-start | bytes 23048 | tf_op jit(solution)/shard_map/ppermute | solution.py:25
  40.7 0.8 collective-permute-done.9
  41.5 0.1 maximum_maximum_fusion.1
  41.6 0.2 fusion.13
  41.8 0.6 concatenate.20
  42.5 0.6 copy-done.6
  43.1 0.3 fusion.5
  43.5 1.6 %collective-permute-start.11 = (bf16[8,48,48]{2,1,0:T(8,128)(2,1)S(1)}, bf16[8,48,48]{2,1,0:T(8,128)(2,1)S(1)}, u32[]{:S(2)}, u32[]{:S(2)}) collective-permute-start(bf16[8,48,48]{2,1,0:T(8,128)(2,1)S(1)} %get-tuple-element.29), channel_id=1, source_target_pairs={{0,2},{2,4},{4,6},{6,8},{8,10},{10,12},{12,14},{1,3},{3,5},{5,7},{... | collective-permute-start | bytes 110600 | tf_op jit(solution)/shard_map/ppermute | solution.py:25
  45.1 1.3 %collective-permute-start.12 = (bf16[8,48,48]{2,1,0:T(8,128)(2,1)S(1)}, bf16[8,48,48]{2,1,0:T(8,128)(2,1)S(1)}, u32[]{:S(2)}, u32[]{:S(2)}) collective-permute-start(bf16[8,48,48]{2,1,0:T(8,128)(2,1)S(1)} %get-tuple-element.30), channel_id=1, source_target_pairs={{2,0},{4,2},{6,4},{8,6},{10,8},{12,10},{14,12},{3,1},{5,3},{7,5},{... | collective-permute-start | bytes 110600 | tf_op jit(solution)/shard_map/ppermute | solution.py:26
  46.4 1.2 %collective-permute-done.11 = bf16[8,48,48]{2,1,0:T(8,128)(2,1)S(1)} collective-permute-done((bf16[8,48,48]{2,1,0:T(8,128)(2,1)S(1)}, bf16[8,48,48]{2,1,0:T(8,128)(2,1)S(1)}, u32[]{:S(2)}, u32[]{:S(2)}) %collective-permute-start.11) | collective-permute-done | bytes 36896 | tf_op jit(solution)/shard_map/ppermute | solution.py:25
  47.6 4.1 %collective-permute-done.12 = bf16[8,48,48]{2,1,0:T(8,128)(2,1)S(1)} collective-permute-done((bf16[8,48,48]{2,1,0:T(8,128)(2,1)S(1)}, bf16[8,48,48]{2,1,0:T(8,128)(2,1)S(1)}, u32[]{:S(2)}, u32[]{:S(2)}) %collective-permute-start.12) | collective-permute-done | bytes 36896 | tf_op jit(solution)/shard_map/ppermute | solution.py:26
  51.8 1.3 %collective-permute-start.13 = (bf16[28,8,48]{2,1,0:T(8,128)(2,1)S(1)}, bf16[28,8,48]{2,1,0:T(8,128)(2,1)S(1)}, u32[]{:S(2)}, u32[]{:S(2)}) collective-permute-start(bf16[28,8,48]{2,1,0:T(8,128)(2,1)S(1)} %get-tuple-element.14), channel_id=1, source_target_pairs={{0,1},{2,3},{4,5},{6,7},{8,9},{10,11},{12,13},{14,15},{16,17},{18,... | collective-permute-start | bytes 64520 | tf_op jit(solution)/shard_map/ppermute | solution.py:25
  53.1 1.3 %collective-permute-start.14 = (bf16[28,8,48]{2,1,0:T(8,128)(2,1)S(1)}, bf16[28,8,48]{2,1,0:T(8,128)(2,1)S(1)}, u32[]{:S(2)}, u32[]{:S(2)}) collective-permute-start(bf16[28,8,48]{2,1,0:T(8,128)(2,1)S(1)} %get-tuple-element.15), channel_id=1, source_target_pairs={{1,0},{3,2},{5,4},{7,6},{9,8},{11,10},{13,12},{15,14},{17,16},{19,... | collective-permute-start | bytes 64520 | tf_op jit(solution)/shard_map/ppermute | solution.py:26
  54.4 1.8 %collective-permute-done.14 = bf16[28,8,48]{2,1,0:T(8,128)(2,1)S(1)} collective-permute-done((bf16[28,8,48]{2,1,0:T(8,128)(2,1)S(1)}, bf16[28,8,48]{2,1,0:T(8,128)(2,1)S(1)}, u32[]{:S(2)}, u32[]{:S(2)}) %collective-permute-start.14) | collective-permute-done | bytes 21536 | tf_op jit(solution)/shard_map/ppermute | solution.py:26
  56.3 0.2 fusion.12
  56.5 0.6 concatenate.23
  57.2 0.2 copy-done.2
  57.4 0.4 copy-done.7
  57.9 0.3 fusion.4
  58.4 0.8 reshape.94
  59.2 9.3 %all-to-all-start = ((bf16[8,2,1728]{2,1,0:T(2,128)(2,1)}), bf16[8,2,1728]{2,1,0:T(2,128)(2,1)S(1)}, u32[]{:S(2)}, u32[]{:S(2)}) async-start(bf16[8,2,1728]{2,1,0:T(2,128)(2,1)} %reshape.94), calls=%async_computation | async-start | bytes 114688 | tf_op jit(solution)/shard_map/all_to_all | solution.py:122
  68.5 6.8 %all-to-all-done = bf16[8,2,1728]{2,1,0:T(2,128)(2,1)S(1)} async-done(((bf16[8,2,1728]{2,1,0:T(2,128)(2,1)}), bf16[8,2,1728]{2,1,0:T(2,128)(2,1)S(1)}, u32[]{:S(2)}, u32[]{:S(2)}) %all-to-all-start) | async-done | bytes 55328 | tf_op jit(solution)/shard_map/all_to_all | solution.py:122
  75.4 0.2 reshape.95
  75.6 0.2 reshape.96
  75.8 3.8 %all_to_all.10 = bf16[2,2,6912]{2,1,0:T(2,128)(2,1)S(1)} all-to-all(bf16[2,2,6912]{2,1,0:T(2,128)(2,1)S(1)} %reshape.96), channel_id=1, replica_groups=mesh['group'=2,'row'=8,'col'=2] {'col'}, dimensions={0} | all-to-all | bytes 110592 | tf_op jit(solution)/shard_map/all_to_all | solution.py:121
  79.6 0.2 reshape.97
  80.0 0.6 collective-permute-start.15
  80.5 6.0 %collective-permute-done.15 = bf16[4,6,12,48]{3,0,2,1:T(4,128)(2,1)S(1)} collective-permute-done((bf16[4,6,12,48]{3,0,2,1:T(4,128)(2,1)S(1)}, bf16[4,6,12,48]{3,0,2,1:T(4,128)(2,1)S(1)}, u32[]{:S(2)}, u32[]{:S(2)}) %collective-permute-start.15) | collective-permute-done | bytes 27680 | tf_op jit(solution)/shard_map/ppermute | solution.py:34
  86.6 0.2 convert_bitcast_fusion
  86.7 0.2 copy.25
  87.0 0.6 copy-done.8
  87.6 0.9 %fusion.6 = f32[12,48]{1,0:T(8,128)} fusion(f32[12,48,48]{2,1,0:T(8,128)S(1)} %reshape.82, bf16[12,48,48]{2,1,0:T(8,128)(2,1)S(1)} %fusion.4, f32[48]{0:T(128)S(1)} %copy-done.9, f32[48]{0:T(128)S(1)} %copy-done.10, bf16[48,48]{1,0:T(8,128)(2,1)S(1)} %copy-done.8), kind=kOutput, calls=%fused_computation.10 | convolution fusion | flops 2874816 | bytes 173184 | tf_op jit(solution)/shard_map/rch,hk->rck/dot_general | solution.py:141
  (51 shorter events, 1.1 us)
Async XLA Ops:
  0.0 42.5 %copy-start = (bf16[3,3,48,48]{3,2,1,0:T(8,128)(2,1)S(1)}, bf16[3,3,48,48]{3,2,1,0:T(8,128)(2,1)}, u32[]{:S(2)}) copy-start(bf16[3,3,48,48]{3,2,1,0:T(8,128)(2,1)} %param.15) | copy-start | bytes 124420
  0.0 7.8 %collective-permute-start = (bf16[12,96]{1,0:T(8,128)(2,1)}, bf16[12,96]{1,0:T(8,128)(2,1)S(1)}, u32[]{:S(2)}, u32[]{:S(2)}) collective-permute-start(bf16[12,96]{1,0:T(8,128)(2,1)} %param.12), channel_id=1, source_target_pairs={{0,2},{2,4},{4,6},{6,8},{8,10},{10,12},{12,14},{14,0},{1,3},{3,5},... | collective-permute-start | bytes 6920 | tf_op jit(solution)/shard_map/ppermute | solution.py:76
  7.8 6.3 %collective-permute-start.1 = (bf16[12,96]{1,0:T(8,128)(2,1)S(1)}, bf16[12,96]{1,0:T(8,128)(2,1)S(1)}, u32[]{:S(2)}, u32[]{:S(2)}) collective-permute-start(bf16[12,96]{1,0:T(8,128)(2,1)S(1)} %collective-permute-done), channel_id=1, source_target_pairs={{0,2},{2,4},{4,6},{6,8},{8,10},{10,12},{12,14},{14,0},{1,3},{3,5},... | collective-permute-start | bytes 6920 | tf_op jit(solution)/shard_map/ppermute | solution.py:76
  7.8 6.3 %collective-permute-start.4 = (bf16[12,96]{1,0:T(8,128)(2,1)}, bf16[12,96]{1,0:T(8,128)(2,1)S(1)}, u32[]{:S(2)}, u32[]{:S(2)}) collective-permute-start(bf16[12,96]{1,0:T(8,128)(2,1)} %param.12), channel_id=1, source_target_pairs={{2,0},{4,2},{6,4},{8,6},{10,8},{12,10},{14,12},{0,14},{3,1},{5,3},... | collective-permute-start | bytes 6920 | tf_op jit(solution)/shard_map/ppermute | solution.py:79
  14.1 6.3 %collective-permute-start.2 = (bf16[12,96]{1,0:T(8,128)(2,1)S(1)}, bf16[12,96]{1,0:T(8,128)(2,1)S(1)}, u32[]{:S(2)}, u32[]{:S(2)}) collective-permute-start(bf16[12,96]{1,0:T(8,128)(2,1)S(1)} %collective-permute-done.1), channel_id=1, source_target_pairs={{0,2},{2,4},{4,6},{6,8},{8,10},{10,12},{12,14},{14,0},{1,3},{3,5},... | collective-permute-start | bytes 6920 | tf_op jit(solution)/shard_map/ppermute | solution.py:76
  14.1 6.3 %collective-permute-start.5 = (bf16[12,96]{1,0:T(8,128)(2,1)S(1)}, bf16[12,96]{1,0:T(8,128)(2,1)S(1)}, u32[]{:S(2)}, u32[]{:S(2)}) collective-permute-start(bf16[12,96]{1,0:T(8,128)(2,1)S(1)} %collective-permute-done.4), channel_id=1, source_target_pairs={{2,0},{4,2},{6,4},{8,6},{10,8},{12,10},{14,12},{0,14},{3,1},{5,3},... | collective-permute-start | bytes 6920 | tf_op jit(solution)/shard_map/ppermute | solution.py:79
  20.4 6.3 %collective-permute-start.3 = (bf16[12,96]{1,0:T(8,128)(2,1)S(1)}, bf16[12,96]{1,0:T(8,128)(2,1)S(1)}, u32[]{:S(2)}, u32[]{:S(2)}) collective-permute-start(bf16[12,96]{1,0:T(8,128)(2,1)S(1)} %collective-permute-done.2), channel_id=1, source_target_pairs={{0,2},{2,4},{4,6},{6,8},{8,10},{10,12},{12,14},{14,0},{1,3},{3,5},... | collective-permute-start | bytes 6920 | tf_op jit(solution)/shard_map/ppermute | solution.py:76
  20.4 7.0 %collective-permute-start.6 = (bf16[12,96]{1,0:T(8,128)(2,1)S(1)}, bf16[12,96]{1,0:T(8,128)(2,1)S(1)}, u32[]{:S(2)}, u32[]{:S(2)}) collective-permute-start(bf16[12,96]{1,0:T(8,128)(2,1)S(1)} %collective-permute-done.5), channel_id=1, source_target_pairs={{2,0},{4,2},{6,4},{8,6},{10,8},{12,10},{14,12},{0,14},{3,1},{5,3},... | collective-permute-start | bytes 6920 | tf_op jit(solution)/shard_map/ppermute | solution.py:79
  26.7 0.7 copy-start.5
  27.4 0.7 copy-start.3
  27.4 0.8 copy-start.4
  28.0 0.9 %copy-start.1 = (bf16[12,48,48]{2,1,0:T(8,128)(2,1)S(1)}, bf16[12,48,48]{2,1,0:T(8,128)(2,1)}, u32[]{:S(2)}) copy-start(bf16[12,48,48]{2,1,0:T(8,128)(2,1)} %param.11) | copy-start | bytes 165892
  29.0 3.0 %collective-permute-start.7 = (bf16[4,48,48]{2,1,0:T(8,128)(2,1)S(1)}, bf16[4,48,48]{2,1,0:T(8,128)(2,1)S(1)}, u32[]{:S(2)}, u32[]{:S(2)}) collective-permute-start(bf16[4,48,48]{2,1,0:T(8,128)(2,1)S(1)} %get-tuple-element.31), channel_id=1, source_target_pairs={{0,2},{2,4},{4,6},{6,8},{8,10},{10,12},{12,14},{1,3},{3,5},{5,7},{... | collective-permute-start | bytes 55304 | tf_op jit(solution)/shard_map/ppermute | solution.py:25
  30.3 6.0 %collective-permute-start.8 = (bf16[4,48,48]{2,1,0:T(8,128)(2,1)S(1)}, bf16[4,48,48]{2,1,0:T(8,128)(2,1)S(1)}, u32[]{:S(2)}, u32[]{:S(2)}) collective-permute-start(bf16[4,48,48]{2,1,0:T(8,128)(2,1)S(1)} %get-tuple-element.32), channel_id=1, source_target_pairs={{2,0},{4,2},{6,4},{8,6},{10,8},{12,10},{14,12},{3,1},{5,3},{7,5},{... | collective-permute-start | bytes 55304 | tf_op jit(solution)/shard_map/ppermute | solution.py:26
  36.3 4.3 %collective-permute-start.10 = (bf16[20,4,48]{2,1,0:T(4,128)(2,1)S(1)}, bf16[20,4,48]{2,1,0:T(4,128)(2,1)S(1)}, u32[]{:S(2)}, u32[]{:S(2)}) collective-permute-start(bf16[20,4,48]{2,1,0:T(4,128)(2,1)S(1)} %get-tuple-element.26), channel_id=1, source_target_pairs={{1,0},{3,2},{5,4},{7,6},{9,8},{11,10},{13,12},{15,14},{17,16},{19,... | collective-permute-start | bytes 23048 | tf_op jit(solution)/shard_map/ppermute | solution.py:26
  37.6 3.9 %collective-permute-start.9 = (bf16[20,4,48]{2,1,0:T(4,128)(2,1)S(1)}, bf16[20,4,48]{2,1,0:T(4,128)(2,1)S(1)}, u32[]{:S(2)}, u32[]{:S(2)}) collective-permute-start(bf16[20,4,48]{2,1,0:T(4,128)(2,1)S(1)} %get-tuple-element.25), channel_id=1, source_target_pairs={{0,1},{2,3},{4,5},{6,7},{8,9},{10,11},{12,13},{14,15},{16,17},{18,... | collective-permute-start | bytes 23048 | tf_op jit(solution)/shard_map/ppermute | solution.py:25
  42.5 0.7 copy-start.6
  43.5 4.1 %collective-permute-start.11 = (bf16[8,48,48]{2,1,0:T(8,128)(2,1)S(1)}, bf16[8,48,48]{2,1,0:T(8,128)(2,1)S(1)}, u32[]{:S(2)}, u32[]{:S(2)}) collective-permute-start(bf16[8,48,48]{2,1,0:T(8,128)(2,1)S(1)} %get-tuple-element.29), channel_id=1, source_target_pairs={{0,2},{2,4},{4,6},{6,8},{8,10},{10,12},{12,14},{1,3},{3,5},{5,7},{... | collective-permute-start | bytes 110600 | tf_op jit(solution)/shard_map/ppermute | solution.py:25
  45.1 6.7 %collective-permute-start.12 = (bf16[8,48,48]{2,1,0:T(8,128)(2,1)S(1)}, bf16[8,48,48]{2,1,0:T(8,128)(2,1)S(1)}, u32[]{:S(2)}, u32[]{:S(2)}) collective-permute-start(bf16[8,48,48]{2,1,0:T(8,128)(2,1)S(1)} %get-tuple-element.30), channel_id=1, source_target_pairs={{2,0},{4,2},{6,4},{8,6},{10,8},{12,10},{14,12},{3,1},{5,3},{7,5},{... | collective-permute-start | bytes 110600 | tf_op jit(solution)/shard_map/ppermute | solution.py:26
  51.8 2.6 %collective-permute-start.13 = (bf16[28,8,48]{2,1,0:T(8,128)(2,1)S(1)}, bf16[28,8,48]{2,1,0:T(8,128)(2,1)S(1)}, u32[]{:S(2)}, u32[]{:S(2)}) collective-permute-start(bf16[28,8,48]{2,1,0:T(8,128)(2,1)S(1)} %get-tuple-element.14), channel_id=1, source_target_pairs={{0,1},{2,3},{4,5},{6,7},{8,9},{10,11},{12,13},{14,15},{16,17},{18,... | collective-permute-start | bytes 64520 | tf_op jit(solution)/shard_map/ppermute | solution.py:25
  53.1 3.1 %collective-permute-start.14 = (bf16[28,8,48]{2,1,0:T(8,128)(2,1)S(1)}, bf16[28,8,48]{2,1,0:T(8,128)(2,1)S(1)}, u32[]{:S(2)}, u32[]{:S(2)}) collective-permute-start(bf16[28,8,48]{2,1,0:T(8,128)(2,1)S(1)} %get-tuple-element.15), channel_id=1, source_target_pairs={{1,0},{3,2},{5,4},{7,6},{9,8},{11,10},{13,12},{15,14},{17,16},{19,... | collective-permute-start | bytes 64520 | tf_op jit(solution)/shard_map/ppermute | solution.py:26
  56.5 0.9 %copy-start.2 = (bf16[3,3,48,48]{3,2,1,0:T(8,128)(2,1)S(1)}, bf16[3,3,48,48]{3,2,1,0:T(8,128)(2,1)}, u32[]{:S(2)}) copy-start(bf16[3,3,48,48]{3,2,1,0:T(8,128)(2,1)} %param.17) | copy-start | bytes 124420
  57.2 0.7 copy-start.7
  59.2 16.2 %all-to-all-start = ((bf16[8,2,1728]{2,1,0:T(2,128)(2,1)}), bf16[8,2,1728]{2,1,0:T(2,128)(2,1)S(1)}, u32[]{:S(2)}, u32[]{:S(2)}) async-start(bf16[8,2,1728]{2,1,0:T(2,128)(2,1)} %reshape.94), calls=%async_computation | async-start | bytes 114688 | tf_op jit(solution)/shard_map/all_to_all | solution.py:122
  80.0 6.6 %collective-permute-start.15 = (bf16[4,6,12,48]{3,0,2,1:T(4,128)(2,1)S(1)}, bf16[4,6,12,48]{3,0,2,1:T(4,128)(2,1)S(1)}, u32[]{:S(2)}, u32[]{:S(2)}) collective-permute-start(bf16[4,6,12,48]{3,0,2,1:T(4,128)(2,1)S(1)} %get-tuple-element.28), channel_id=1, source_target_pairs={{0,8},{2,10},{4,12},{6,14},{8,0},{10,2},{12,4},{14,6},{1,9},{3,11}... | collective-permute-start | bytes 82952 | tf_op jit(solution)/shard_map/ppermute | solution.py:34
  86.9 0.7 copy-start.8
  86.9 0.7 copy-start.9
  86.9 0.7 copy-start.10
